TPU v7x, 512 devices: a whole 4x8x8 slice. The times are simulated.
512 devices in a mesh: tm: 8 (over z_hi, core), height: 8 (over x, z_lo), head: 8 (over y).
Axes of the slice: x: 4, y: 8, z: 8 (z_hi: 4, z_lo: 2; z = z_hi * 2 + z_lo), core: 2. Of those that a mesh axis runs over, the one named last changes fastest.
Arguments:
- lat_q: bfloat16 [8, 8, 2, 384, 3072], P('tm', 'height', None, None, 'head'), may hold values from -12 to 12
- lat_kv: bfloat16 [2, 8, 8, 2, 384, 3072], P(None, 'tm', 'height', None, None, 'head'), may hold values from -6 to 6
- txt_qkv: bfloat16 [3, 64, 128, 3072], P(None, ('tm', 'height'), None, 'head'), may hold values from -12 to 12
- blocks: int32 [8, 8, 2, 9], P('tm', 'height'), may hold values from -1 to 127, as said below
- owner: int32 [8], P('head'), may hold values from 0 to 63
Outputs:
- latent_out: bfloat16 [8, 8, 2, 384, 3072], P('tm', 'height', None, None, 'head')
- text_out: bfloat16 [128, 3072], P(None, 'head')
Inputs may be any that keep to these rules, and one draw needn't show every extreme that they name: `blocks`: row i lists its own tile i first, then distinct tiles with the same width index whose frame and height tile indices each differ from tile i's by at most one, then -1 entries; some row lists 9 tiles.
All inputs are finite; a program needn't handle non-finite values.
Results may differ from a plain program's by a relative error of at most 0.0031.
Values may be sent and summed in bfloat16 or wider, within the bound.
No kernel may reach another device: no remote copies, remote signals or barrier semaphores. Data moves between devices by JAX's collectives and lax.ppermute only.
A program may use at most 128 MiB of HBM per device.

v0:
```python
import jax
import jax.numpy as jnp
from jax import lax
from jax.sharding import PartitionSpec as P

HD = 128


def broadcast(value, axis, source):
    kept = jnp.where(lax.axis_index(axis) == source, value, 0).astype(value.dtype)
    return lax.psum(kept, axis)


def padded(x, sides, width):
    for axis, dim in sides:
        count, length = (lax.axis_size(axis), x.shape[dim])
        up = [(i, (i + 1) % count) for i in range(count - 1)]
        down = [(j, i) for i, j in up]
        last = lax.slice_in_dim(x, length - width, length, axis=dim)
        initial = lax.slice_in_dim(x, 0, width, axis=dim)
        before = lax.ppermute(last, axis, up)
        after = lax.ppermute(initial, axis, down)
        x = jnp.concatenate([before, x, after], axis=dim)
    return x


def combined_all(part, axis, combine):
    gathered = jax.tree.map(lambda a: lax.all_gather(a, axis), part)

    def take(source):
        return jax.tree.map(lambda a: lax.dynamic_index_in_dim(a, source, 0, False), gathered)

    return lax.fori_loop(
        1, lax.axis_size(axis), lambda source, state: combine(state, take(source)), take(0)
    )


def combine(first, second):
    max_first, sum_first, acc_first = first
    max_second, sum_second, acc_second = second
    merged_max = jnp.maximum(max_first, max_second)
    factor_first = jnp.exp(max_first - merged_max)
    factor_second = jnp.exp(max_second - merged_max)
    merged_sum = sum_first * factor_first + sum_second * factor_second
    merged_acc = acc_first * factor_first[..., None] + acc_second * factor_second[..., None]
    return (merged_max, merged_sum, merged_acc)


def text_part(head, text_query, key_block, value_block, inv_root):
    head_query = lax.dynamic_slice_in_dim(text_query, head * HD, HD, 1)
    head_key = lax.dynamic_slice_in_dim(key_block, head * HD, HD, 1)
    head_value = lax.dynamic_slice_in_dim(value_block, head * HD, HD, 1)
    scores = (
        jnp.einsum("qd,kd->qk", head_query, head_key, preferred_element_type=jnp.float32) * inv_root
    )
    row_max = jnp.max(scores, axis=1)
    weights = jnp.exp(scores - row_max[:, None])
    weighted = jnp.dot(weights, head_value, precision=lax.Precision.HIGHEST)
    return (row_max, jnp.sum(weights, axis=1), weighted)


def body(lat_q, lat_kv, txt_qkv, blocks, owner):
    column_count = lat_q.shape[-1]
    head_count = column_count // HD
    width_tiles = lat_q.shape[2]
    tile_rows = lat_q.shape[3]
    list_length = blocks.shape[-1]
    text_count = txt_qkv.shape[2]
    inv_root = HD ** (-0.5)
    owner_text = broadcast(txt_qkv, ("tm", "height"), owner[0])
    text_query = owner_text[0, 0]
    text_key = owner_text[1, 0]
    text_value = owner_text[2, 0]
    extended = padded(lat_kv, (("tm", 1), ("height", 2)), 1)
    near_keys = extended[0].reshape(9 * width_tiles, tile_rows, column_count)
    near_values = extended[1].reshape(9 * width_tiles, tile_rows, column_count)
    my_time = lax.axis_index("tm")
    my_height = lax.axis_index("height")
    height_count = lax.axis_size("height")
    tile_outputs = []
    for width_index in range(width_tiles):
        tile_ids = blocks[0, 0, width_index]
        listed = tile_ids >= 0
        clamped = jnp.maximum(tile_ids, 0)
        key_time = clamped // (height_count * width_tiles)
        key_height = clamped // width_tiles % height_count
        key_width = clamped % width_tiles
        position = (
            (key_time - my_time + 1) * 3 + (key_height - my_height + 1)
        ) * width_tiles + key_width
        position = jnp.where(listed, position, 0)
        key_rows = jnp.concatenate(
            [near_keys[position].reshape(list_length * tile_rows, column_count), text_key], 0
        )
        value_rows = jnp.concatenate(
            [near_values[position].reshape(list_length * tile_rows, column_count), text_value], 0
        )
        key_bias = jnp.concatenate(
            [
                jnp.repeat(jnp.where(listed, 0.0, -1e30).astype(jnp.float32), tile_rows),
                jnp.zeros((text_count,), jnp.float32),
            ]
        )
        queries = lat_q[0, 0, width_index]

        def one_head(head):
            head_query = lax.dynamic_slice_in_dim(queries, head * HD, HD, 1)
            head_key = lax.dynamic_slice_in_dim(key_rows, head * HD, HD, 1)
            head_value = lax.dynamic_slice_in_dim(value_rows, head * HD, HD, 1)
            scores = (
                jnp.einsum("qd,kd->qk", head_query, head_key, preferred_element_type=jnp.float32)
                * inv_root
                + key_bias[None, :]
            )
            row_max = jnp.max(scores, axis=1, keepdims=True)
            weights = jnp.exp(scores - row_max)
            row_sum = jnp.sum(weights, axis=1, keepdims=True)
            mixed = (
                jnp.dot(
                    weights.astype(jnp.bfloat16), head_value, preferred_element_type=jnp.float32
                )
                / row_sum
            )
            return mixed.astype(jnp.bfloat16)

        per_head = lax.map(one_head, jnp.arange(head_count, dtype=jnp.int32))
        tile_outputs.append(jnp.transpose(per_head, (1, 0, 2)).reshape(tile_rows, column_count))
    latent_out = jnp.stack(tile_outputs)[None, None]
    own_keys = lat_kv[0, 0, 0].reshape(width_tiles * tile_rows, column_count)
    own_values = lat_kv[1, 0, 0].reshape(width_tiles * tile_rows, column_count).astype(jnp.float32)

    def partial_head(head):
        return text_part(head, text_query, own_keys, own_values, inv_root)

    part_max, part_sum, part_acc = lax.map(partial_head, jnp.arange(head_count, dtype=jnp.int32))
    part_max, part_sum, part_acc = combined_all(
        (part_max, part_sum, part_acc), ("tm", "height"), combine
    )
    text_value_wide = text_value.astype(jnp.float32)

    def text_head(head):
        return text_part(head, text_query, text_key, text_value_wide, inv_root)

    own_text = lax.map(text_head, jnp.arange(head_count, dtype=jnp.int32))
    final_max, final_sum, final_acc = combine((part_max, part_sum, part_acc), own_text)
    text_mixed = final_acc / final_sum[..., None]
    text_out = (
        jnp.transpose(text_mixed, (1, 0, 2)).reshape(text_count, column_count).astype(jnp.bfloat16)
    )
    return (latent_out, text_out)


def solution(mesh):
    placed = (
        P("tm", "height", None, None, "head"),
        P(None, "tm", "height", None, None, "head"),
        P(None, ("tm", "height"), None, "head"),
        P("tm", "height", None, None),
        P("head"),
    )
    return jax.shard_map(
        body,
        mesh=mesh,
        in_specs=placed,
        out_specs=(P("tm", "height", None, None, "head"), P(None, "head")),
        check_vma=False,
    )
```

profile of v0, /device:TPU:56, one launch (start us, length us, event | category | flops | bytes accessed | tf_op | source)
XLA Modules:
  0.0 941.4 jit_solution(2615295721121671516)
XLA Ops:
  11.2 194.6 %all-reduce.4.cloned.1.call-done = bf16[3,1,128,384]{3,2,1,0:T(8,128)(2,1)} async-done(((bf16[3,1,128,384]{3,2,1,0:T(8,128)(2,1)}), bf16[3,1,128,384]{3,2,1,0:T(8,128)(2,1)}) %all-reduce.4.cloned.1.call-update) | async-done | bytes 294928 | tf_op jit(solution)/shard_map/psum | solution.py:11
  207.5 9.2 while.69
  216.7 1.9 collective-permute-start
  224.3 4.7 collective-permute-start.2
  238.1 1.9 slice_bitcast_fusion.1
  240.1 295.7 %all-gather.4 = f32[64,3,128]{2,1,0:T(4,128)S(1)} all-gather(f32[1,3,128]{2,1,0:T(4,128)} %bitcast.216), channel_id=3, replica_groups=mesh['tm'=8,'height'=8,'head'=8] {'tm','height'}, dimensions={0}, use_global_device_ids=true | all-gather | bytes 99840 | tf_op jit(solution)/shard_map/all_gather | solution.py:28
  535.8 124.9 %all-gather.3 = f32[64,3,128]{2,1,0:T(4,128)S(1)} all-gather(f32[1,3,128]{2,1,0:T(4,128)} %bitcast.215), channel_id=2, replica_groups=mesh['tm'=8,'height'=8,'head'=8] {'tm','height'}, dimensions={0}, use_global_device_ids=true | all-gather | bytes 99840 | tf_op jit(solution)/shard_map/all_gather | solution.py:28
  663.5 23.0 %while.71 = (s32[]{:T(128)}, f32[3,128]{1,0:T(4,128)}, f32[3,128]{1,0:T(4,128)}, f32[3,128,128]{1,2,0:T(8,128)}, s32[3]{0:T(128)}, /*index=5*/bf16[128,384]{1,0:...) while((s32[]{:T(128)}, f32[3,128]{1,0:T(4,128)}, ...), condition=%wide.region_18.19_spmd, body=%wide.region_15.18_spmd.sunk | while | flops 29441796 | bytes 401111 | solution.py:144
  674.0 1.8 fusion.128
  681.7 1.8 fusion.128
  686.5 8.3 pad_maximum_fusion
  694.8 9.8 %fusion.87 = (bf16[1,3,3,2,384,384]{5,4,3,2,1,0:T(8,128)(2,1)}, bf16[1,3,3,2,384,384]{5,4,3,2,1,0:T(8,128)(2,1)}) fusion(bf16[2,3,3,2,384,384]{5,4,3,2,1,0:T(8,128)(2,1)} %pad_maximum_fusion), kind=kLoop, calls=%fused_computation.133 | loop fusion | bytes 21233664 | tf_op jit(solution)/shard_map/slice | solution.py:76
  704.5 5.4 gather_fusion.1
  710.0 5.3 gather_fusion.3
  715.3 5.4 gather_fusion.2
  720.7 5.3 gather_fusion
  726.0 10.2 %pad_maximum_fusion.2 = (bf16[3584,384]{1,0:T(8,128)(2,1)}, bf16[3584,384]{1,0:T(8,128)(2,1)S(1)}, bf16[3584,384]{1,0:T(8,128)(2,1)}, bf16[3584,384]{1,0:T(8,128)(2,1)}) fusion(bf16[128,384]{1,0:T(8,128)(2,1)S(1)} %copy-done.2, bf16[3456,384]{1,0:T(8,128)(2,1)} %bitcast.205, bf16[3456,384]{1,0:T(8,128)(2,1)} %bitcast.204, bf16[128,384]{1,0:T(8,128)(2,1)S(1)} %copy-done.3, ...), kind=kLoop, calls=%fused_computation.68 | loop fusion | flops 19267584 | bytes 21823488 | tf_op jit(solution)/shard_map/concatenate | solution.py:92
  736.2 20.0 %while.67 = (s32[]{:T(128)}, bf16[3,384,128]{1,2,0:T(8,128)(2,1)S(1)}, s32[3]{0:T(128)S(1)}, bf16[384,384]{1,0:T(8,128)(2,1)}, bf16[3584,384]{1,0:T(8,128)(2,1)}...) while((s32[]{:T(128)}, ...), condition=%wide.region_4.5_spmd, body=%wide.region_1.4_spmd.sunk | while | flops 714374400 | bytes 18963120 | solution.py:126
  737.5 2.2 fusion.111
  740.6 2.1 fusion.113
  744.2 2.3 fusion.111
  747.3 2.1 fusion.113
  750.8 2.2 fusion.111
  754.0 2.1 fusion.113
  756.8 21.2 %while.68 = (s32[]{:T(128)}, bf16[3,384,128]{1,2,0:T(8,128)(2,1)S(1)}, s32[3]{0:T(128)}, bf16[384,384]{1,0:T(8,128)(2,1)}, bf16[3584,384]{1,0:T(8,128)(2,1)S(1)}...) while((s32[]{:T(128)}, ...), condition=%wide.region_8.9_spmd, body=%wide.region_5.8_spmd.sunk | while | flops 714374400 | bytes 18965168 | solution.py:126
  758.9 1.9 fusion.116
  761.7 2.1 fusion.118
  765.9 1.9 fusion.116
  768.7 2.1 fusion.118
  772.9 1.9 fusion.116
  775.7 2.1 fusion.118
  780.1 152.8 %while.70 = (s32[]{:T(128)}, f32[3,128]{1,0:T(4,128)}, f32[3,128]{1,0:T(4,128)}, f32[3,128,128]{2,1,0:T(8,128)S(1)}, f32[64,3,128]{2,1,0:T(4,128)}, /*index=5*/f...) while((s32[]{:T(128)}, f32[3,128]{1,0:T(4,128)}, ...), condition=%wide.region_14.15_spmd, body=%wide.region_13.14_spmd.sunk | while | flops 149765 | bytes 605335 | solution.py:33
  (263 shorter events, 214.5 us)
Async XLA Ops:
  7.2 198.6 %all-reduce.4.cloned.1.call-start = ((), (), s32[]{:S(2)}) async-start(), calls=%async_computation | async-start | bytes 589824 | tf_op jit(solution)/shard_map/psum | solution.py:11
  9.6 769.6 %all-gather.7.cloned.1.call-start = ((), (), s32[]{:S(2)}) async-start(), calls=%async_computation.1 | async-start | bytes 12779520 | tf_op jit(solution)/shard_map/all_gather | solution.py:28
  216.7 3.3 copy-start.1
  216.7 3.3 copy-start.8
  216.7 3.3 copy-start.9
  216.7 13.6 %copy-start.12 = (s32[1,1,2,9]{3,2,1,0:T(2,128)S(1)}, s32[1,1,2,9]{3,2,1,0:T(2,128)}, u32[]{:S(2)}) copy-start(s32[1,1,2,9]{3,2,1,0:T(2,128)} %param.18) | copy-start | bytes 220
  216.7 4.5 collective-permute-start
  218.7 5.3 collective-permute-start.1
  224.3 462.3 %collective-permute-start.2 = (bf16[2,3,1,2,384,384]{5,4,3,2,1,0:T(8,128)(2,1)S(1)}, bf16[2,3,1,2,384,384]{5,4,3,2,1,0:T(8,128)(2,1)}, u32[]{:S(2)}, u32[]{:S(2)}) collective-permute-start(bf16[2,3,1,2,384,384]{5,4,3,2,1,0:T(8,128)(2,1)S(1)} %constant_dynamic-update-slice_fusion.2), channel_id=1, source_target_pairs={{0,8},{8,16},{16,24},{24,32},{32,40},{40,48},{48,56},{1,9},{9,17},... | collective-permute-start | bytes 10616840 | tf_op jit(solution)/shard_map/ppermute | solution.py:21
  229.0 457.5 %collective-permute-start.3 = (bf16[2,3,1,2,384,384]{5,4,3,2,1,0:T(8,128)(2,1)S(1)}, bf16[2,3,1,2,384,384]{5,4,3,2,1,0:T(8,128)(2,1)}, u32[]{:S(2)}, u32[]{:S(2)}) collective-permute-start(bf16[2,3,1,2,384,384]{5,4,3,2,1,0:T(8,128)(2,1)S(1)} %constant_dynamic-update-slice_fusion.2), channel_id=1, source_target_pairs={{8,0},{16,8},{24,16},{32,24},{40,32},{48,40},{56,48},{9,1},{17,9},... | collective-permute-start | bytes 10616840 | tf_op jit(solution)/shard_map/ppermute | solution.py:22
  535.8 124.9 %copy-start.6 = (f32[64,3,128]{2,1,0:T(4,128)}, f32[64,3,128]{2,1,0:T(4,128)S(1)}, u32[]{:S(2)}) copy-start(f32[64,3,128]{2,1,0:T(4,128)S(1)} %all-gather.4) | copy-start | bytes 294916
  660.6 0.7 copy-start.7
  666.3 2.3 copy-start.4
  674.0 2.3 copy-start.4
  681.7 2.3 copy-start.4
  720.7 5.3 copy-start.2
  720.7 5.3 copy-start.3
  726.0 10.2 %copy-start = (f32[3584]{0:T(1024)S(1)}, f32[3584]{0:T(1024)}, u32[]{:S(2)}) copy-start(f32[3584]{0:T(1024)} %concatenate.27) | copy-start | bytes 43012
  778.0 155.0 %copy-start.10 = (f32[3,128]{1,0:T(4,128)S(1)}, f32[3,128]{1,0:T(4,128)}, u32[]{:S(2)}) copy-start(f32[3,128]{1,0:T(4,128)} %get-tuple-element.349) | copy-start | bytes 4612
  778.0 155.0 %copy-start.11 = (f32[3,128]{1,0:T(4,128)S(1)}, f32[3,128]{1,0:T(4,128)}, u32[]{:S(2)}) copy-start(f32[3,128]{1,0:T(4,128)} %get-tuple-element.352) | copy-start | bytes 4612
  778.0 155.7 %copy-start.5 = (f32[3,128,128]{1,2,0:T(8,128)S(1)}, f32[3,128,128]{1,2,0:T(8,128)}, u32[]{:S(2)}) copy-start(f32[3,128,128]{1,2,0:T(8,128)} %get-tuple-element.350) | copy-start | bytes 589828
Sparse Core Ops, SparseCore 0:
  12.0 193.7 all-reduce.3
  216.8 320.7 all-gather.6
where the time goes:
time: 958 us; the launch traced here: 941 us
  blocking collectives  421 us (44%)
  waiting for transfers between devices  197 us (21%)
  other arithmetic  184 us (19%)
  local copies, waits for them, and re-layouts  67.8 us (7%)
  matrix products  37.9 us (4%)
  between operations  14.9 us (2%)
  loops' own time  9.84 us (1%)
    all_gather x2, blocking collectives, combined_all(): gathered = jax.tree.map(lambda a: lax.all_gather(a, axis), part)  421 us
    psum x1, waiting for transfers between devices, broadcast(): return lax.psum(kept, axis)  195 us
    add x64, other arithmetic, combine(): merged_sum = sum_first * factor_first + sum_second * factor_second  80.8 us
    add x63, other arithmetic, combine(): acc_first * factor_first[..., None] + acc_second * factor_second[..., None]  71.1 us
  transfers between devices with their start and end apart: 6, of which 3 were waited for; matrix products, arithmetic and copies ran while one was open for 13% of the time, Pallas kernels for 0%

commit v1 on v0

v1 whole, which is shorter than its diff:
```python
import functools

import jax
import jax.numpy as jnp
from jax import lax
from jax.experimental import pallas as pl
from jax.experimental.pallas import tpu as pltpu
from jax.sharding import Mesh, PartitionSpec as P

HD = 128
LOG2E = 1.4426950408889634
FAR_AWAY = 1e30

AX = ("zh", "core", "x", "zl")
SIZES = (4, 2, 4, 2)
ROWS16 = ("core", "x", "zl")


def flat(place):
    out = 0
    for size, part in zip(SIZES, place):
        out = out * size + part
    return out


def pairs(rule):
    found = []
    for zh in range(SIZES[0]):
        for core in range(SIZES[1]):
            for x in range(SIZES[2]):
                for zl in range(SIZES[3]):
                    target = rule(zh, core, x, zl)
                    if target is None:
                        continue
                    if all(0 <= part < size for part, size in zip(target, SIZES)):
                        found.append((flat((zh, core, x, zl)), flat(target)))
    return found


SWAP_CORE = pairs(lambda zh, c, x, zl: (zh, 1 - c, x, zl))
SWAP_ZL = pairs(lambda zh, c, x, zl: (zh, c, x, 1 - zl))
X_NEAR = pairs(lambda zh, c, x, zl: (zh, c, x - 1 if zl == 0 else x + 1, zl))
X_FAR = pairs(lambda zh, c, x, zl: (zh, c, x + 1 if zl == 0 else x - 1, zl))
NEXT_BLOCK = pairs(lambda zh, c, x, zl: (zh - 1 if zl == 0 else zh + 1, c, x, 1 - zl))
Q_FIRST = pairs(lambda zh, c, x, zl: (zh, 1 - c, x, zl) if c == zl else (zh, c, x, 1 - zl))
Q_SECOND = pairs(lambda zh, c, x, zl: None if c == zl else (zh, 1 - c, x, 1 - zl))
OUT_NEAR = pairs(lambda zh, c, x, zl: None if c == zl else (zh, 1 - c, x, zl))
OUT_FAR_FIRST = pairs(lambda zh, c, x, zl: (zh, c, x, 1 - zl) if c == zl else None)
OUT_FAR_SECOND = pairs(lambda zh, c, x, zl: None if c == zl else (zh, 1 - c, x, 1 - zl))

SCALE = HD ** (-0.5) * LOG2E


def attend(query, keys_values, carry):
    scores = []
    top = None if carry is None else carry[0]
    for keys, _, bias in keys_values:
        score = lax.dot_general(
            query, keys, (((1,), (1,)), ((), ())), preferred_element_type=jnp.float32
        )
        scores.append(score)
        score_top = jnp.max(score, axis=1, keepdims=True)
        if bias is not None:
            score_top = score_top + bias
        top = score_top if top is None else jnp.maximum(top, score_top)
    total = None
    mixed = None
    if carry is not None:
        factor = jnp.exp2((carry[0] - top) * SCALE)
        total = carry[1] * factor
        mixed = carry[2] * factor
    for score, (_, values, bias) in zip(scores, keys_values):
        shift = top if bias is None else top - bias
        weights = jnp.exp2((score - shift) * SCALE)
        part_total = jnp.sum(weights, axis=1, keepdims=True)
        part = jnp.dot(
            weights.astype(jnp.bfloat16), values, preferred_element_type=jnp.float32
        )
        total = part_total if total is None else total + part_total
        mixed = part if mixed is None else mixed + part
    return top, total, mixed


def bias_of(listed_ref, index):
    return jnp.where(listed_ref[index] > 0, 0.0, -FAR_AWAY).astype(jnp.float32)


def pack_stats(top, total, rows):
    lane = lax.broadcasted_iota(jnp.int32, (rows, HD), 1)
    return jnp.where(lane < HD // 2, top, total)


def block_kernel(near_listed, far_listed, near_q, far_q, pair, far_pair, *outs, rows):
    for listed, query, (stats, acc) in (
        (near_listed, near_q, outs[:2]),
        (far_listed, far_q, outs[2:]),
    ):
        tiles = []
        for index, (ref, tile) in enumerate(((pair, 0), (pair, 1), (far_pair, 0), (far_pair, 1))):
            tiles.append((ref[tile, 0], ref[tile, 1], bias_of(listed, index)))
        top, total, mixed = attend(query[...], tiles, None)
        stats[...] = pack_stats(top, total, rows)
        acc[...] = mixed


def rest_kernel(listed, query, two, *refs, singles, rows):
    ones = refs[:singles]
    text, stats, acc, out = refs[singles:]
    tiles = [(text[1], text[2], None)]
    for tile in range(2):
        tiles.append((two[tile, 0], two[tile, 1], bias_of(listed, 4 + tile)))
    for index, ref in enumerate(ones):
        tiles.append((ref[0], ref[1], bias_of(listed, 6 + index)))
    carry = (stats[:, :1], stats[:, HD // 2 : HD // 2 + 1], acc[...])
    _, total, mixed = attend(query[...], tiles, carry)
    out[...] = (mixed / total).astype(jnp.bfloat16)


def column_block(shape):
    zeros = (0,) * (len(shape) - 1)
    return pl.BlockSpec(tuple(shape[:-1]) + (HD,), lambda head: zeros + (head,))


SMEM = pl.BlockSpec(memory_space=pltpu.SMEM)


def block_attention(near_listed, far_listed, near_q, far_q, pair, far_pair):
    rows, columns = pair.shape[2:]
    state = jax.ShapeDtypeStruct((rows, columns), jnp.float32)
    query_spec = pl.BlockSpec((rows, HD), lambda head: (0, head))
    return pl.pallas_call(
        functools.partial(block_kernel, rows=rows),
        grid=(columns // HD,),
        in_specs=[SMEM, SMEM, query_spec, query_spec]
        + [column_block(pair.shape), column_block(far_pair.shape)],
        out_specs=[query_spec] * 4,
        out_shape=[state] * 4,
        name="block_attention",
    )(near_listed, far_listed, near_q, far_q, pair, far_pair)


def rest_attention(listed, query, two, ones, text, stats, acc, name):
    rows, columns = two.shape[2:]
    query_spec = pl.BlockSpec((rows, HD), lambda head: (0, head))
    return pl.pallas_call(
        functools.partial(rest_kernel, singles=len(ones), rows=rows),
        grid=(columns // HD,),
        in_specs=[SMEM, query_spec, column_block(two.shape)]
        + [column_block(one.shape) for one in ones]
        + [column_block(text.shape), query_spec, query_spec],
        out_specs=query_spec,
        out_shape=jax.ShapeDtypeStruct((rows, columns), jnp.bfloat16),
        name=name,
    )(listed, query, two, *ones, text, stats, acc)


def text_kernel(first, text, kv, acc, stats):
    head = pl.program_id(0)
    query = text[0]
    text_bias = bias_of(first, 0)
    parts = [(text[1], text[2], text_bias), (kv[0, 0], kv[1, 0], None), (kv[0, 1], kv[1, 1], None)]
    scores = []
    top = None
    for keys, _, bias in parts:
        score = lax.dot_general(
            query, keys, (((1,), (1,)), ((), ())), preferred_element_type=jnp.float32
        )
        scores.append(score)
        score_top = jnp.max(score, axis=1, keepdims=True)
        if bias is not None:
            score_top = score_top + bias
        top = score_top if top is None else jnp.maximum(top, score_top)
    total = 0.0
    mixed = 0.0
    for score, (_, values, bias) in zip(scores, parts):
        shift = top if bias is None else top - bias
        weights = jnp.exp2((score - shift) * SCALE)
        total = total + jnp.sum(weights, axis=1, keepdims=True)
        high = weights.astype(jnp.bfloat16)
        low = (weights - high.astype(jnp.float32)).astype(jnp.bfloat16)
        mixed = mixed + jnp.dot(high, values, preferred_element_type=jnp.float32)
        mixed = mixed + jnp.dot(low, values, preferred_element_type=jnp.float32)
    acc[0] = mixed
    lane = lax.broadcasted_iota(jnp.int32, stats.shape, 1)
    heads = pl.num_programs(0)

    @pl.when(head == 0)
    def _():
        stats[...] = jnp.zeros(stats.shape, jnp.float32)

    kept = jnp.where(lane == head, top, stats[...])
    stats[...] = jnp.where(lane == head + heads, total, kept)


def text_partial(first, text, kv):
    count, columns = text.shape[1:]
    heads = columns // HD
    return pl.pallas_call(
        text_kernel,
        grid=(heads,),
        in_specs=[SMEM, column_block(text.shape), column_block(kv.shape)],
        out_specs=[
            pl.BlockSpec((1, count, HD), lambda head: (head, 0, 0)),
            pl.BlockSpec((count, HD), lambda head: (0, 0)),
        ],
        out_shape=[
            jax.ShapeDtypeStruct((heads, count, HD), jnp.float32),
            jax.ShapeDtypeStruct((count, HD), jnp.float32),
        ],
        name="text_partial",
    )(first, text, kv)


def merge_kernel(parts, out, *, heads, queries):
    for row in range(queries):
        stats = parts[:, heads * queries + row, :]
        top = jnp.max(stats, axis=0, keepdims=True)
        factor = jnp.exp2((stats - top) * SCALE)
        for head in range(heads):
            weight = factor[:, head : head + 1]
            total = jnp.sum(
                stats[:, heads + head : heads + head + 1] * weight, axis=0, keepdims=True
            )
            mixed = jnp.sum(parts[:, head * queries + row, :] * weight, axis=0, keepdims=True)
            out[row : row + 1, head * HD : (head + 1) * HD] = mixed / total


def merge_text(parts, heads, queries):
    return pl.pallas_call(
        functools.partial(merge_kernel, heads=heads, queries=queries),
        out_shape=jax.ShapeDtypeStruct((queries, heads * HD), jnp.float32),
        name="merge_text",
    )(parts)


def spread(chunk, axis):
    count = lax.axis_size(axis)
    return lax.all_to_all(jnp.broadcast_to(chunk[None], (count,) + chunk.shape), axis, 0, 0)


def owner_text(txt_qkv, owner):
    kinds, _, count, columns = txt_qkv.shape
    group = lax.axis_size(ROWS16)
    pieces = lax.all_to_all(
        txt_qkv.reshape(group, kinds * count // group, columns), ROWS16, 0, 0
    )
    piece = lax.dynamic_index_in_dim(pieces, owner % group, 0, False)
    piece = lax.dynamic_index_in_dim(spread(piece, "zh"), owner // group, 0, False)
    return spread(piece, ROWS16).reshape(kinds, count, columns)


def listed_slots(ids, slots, width):
    found = []
    for frame, height in slots:
        inside = (frame >= 0) & (frame < 8) & (height >= 0) & (height < 8)
        tile = jnp.where(inside, (frame * 8 + height) * 2 + width, -2)
        found.append(tile)
    return jnp.any(jnp.stack(found)[:, None] == ids[None, :], axis=1).astype(jnp.int32)


def body(lat_q, lat_kv, txt_qkv, blocks, owner):
    zh, core, x, zl = (lax.axis_index(axis) for axis in AX)
    rows, columns = lat_q.shape[3:]
    heads = columns // HD
    list_length = blocks.shape[-1]
    queries = lat_q[0, 0]
    kv = lat_kv[:, 0, 0]
    straight = core == zl
    other = jnp.where(straight, 0, 1)

    text = owner_text(txt_qkv, owner[0])

    kept = lax.dynamic_index_in_dim(kv, core, 1, False)
    given = lax.dynamic_index_in_dim(kv, 1 - core, 1, False)
    received = lax.ppermute(given, AX, SWAP_CORE)
    pair = jnp.stack([kept, received])
    far_pair = lax.ppermute(pair, AX, SWAP_ZL)
    x_near = lax.ppermute(pair, AX, X_NEAR)
    b_far = lax.ppermute(lax.dynamic_index_in_dim(pair, other, 0, False), AX, NEXT_BLOCK)

    ids = jnp.pad(
        blocks[0, 0].astype(jnp.bfloat16), ((0, 0), (0, columns - list_length))
    )[:, None, :]
    asked = jnp.concatenate(
        [queries, ids, jnp.zeros((2, 15, columns), jnp.bfloat16)], axis=1
    )
    q_first = lax.ppermute(lax.dynamic_index_in_dim(asked, 1 - zl, 0, False), AX, Q_FIRST)
    q_second = lax.ppermute(lax.dynamic_index_in_dim(asked, zl, 0, False), AX, Q_SECOND)
    own_q = lax.dynamic_index_in_dim(asked, core, 0, False)
    near_q = jnp.where(straight, own_q, q_first)
    far_q = jnp.where(straight, q_first, q_second)

    x_b_far = lax.ppermute(b_far, AX, X_FAR)
    x_far = lax.ppermute(far_pair, AX, X_FAR)
    b_near = lax.ppermute(lax.dynamic_index_in_dim(far_pair, other, 0, False), AX, NEXT_BLOCK)
    x_b_near = lax.ppermute(b_near, AX, X_NEAR)

    first_frame, second_frame = (2 * zh + core, 2 * zh + 1 - core)
    b_frame = jnp.where(zl == 0, 2 * zh - 1, 2 * zh + 2)
    h_near, h_far = (2 * x + zl, 2 * x + 1 - zl)
    h_x_near = jnp.where(zl == 0, 2 * x + 2, 2 * x - 1)
    h_x_far = jnp.where(zl == 0, 2 * x - 1, 2 * x + 2)
    inner = [
        (first_frame, h_near),
        (second_frame, h_near),
        (first_frame, h_far),
        (second_frame, h_far),
    ]
    beside = [(b_frame, h_far), (b_frame, h_near)]
    near_ids = near_q[rows, :list_length].astype(jnp.int32)
    far_ids = far_q[rows, :list_length].astype(jnp.int32)
    near_listed = listed_slots(
        near_ids,
        inner + [(first_frame, h_x_far), (second_frame, h_x_far)] + beside + [(b_frame, h_x_far)],
        core,
    )
    far_listed = listed_slots(
        far_ids,
        inner + [(first_frame, h_x_near), (second_frame, h_x_near)] + beside + [(b_frame, h_x_near)],
        core,
    )

    near_stats, near_acc, far_stats, far_acc = block_attention(
        near_listed, far_listed, near_q, far_q, pair, far_pair
    )

    first_device = (flat((zh, core, x, zl)) == 0).astype(jnp.int32).reshape(1)
    text_acc, text_stats = text_partial(first_device, text, kv)
    devices = lax.axis_size(AX)
    share = text_acc.shape[1] // devices
    parts = jnp.concatenate(
        [
            jnp.transpose(text_acc.reshape(heads, devices, share, HD), (1, 0, 2, 3)).reshape(
                devices, heads * share, HD
            ),
            text_stats.reshape(devices, share, HD),
        ],
        axis=1,
    )
    merged = merge_text(lax.all_to_all(parts, AX, 0, 0), heads, share)
    text_out = spread(merged.astype(jnp.bfloat16), AX).reshape(text_acc.shape[1], columns)

    far_out = rest_attention(
        far_listed, far_q, x_near, [b_far, b_near, x_b_near], text, far_stats, far_acc, "rest_far"
    )
    back_first = lax.ppermute(far_out, AX, OUT_FAR_FIRST)
    back_second = lax.ppermute(far_out, AX, OUT_FAR_SECOND)
    near_out = rest_attention(
        near_listed, near_q, x_far, [b_far, b_near, x_b_far], text, near_stats, near_acc, "rest_near"
    )
    back_near = lax.ppermute(near_out, AX, OUT_NEAR)
    mine = jnp.where(straight, near_out, back_second)
    theirs = jnp.where(straight, back_near, back_first)
    latent_out = jnp.stack(
        [jnp.where(zl == 0, mine, theirs), jnp.where(zl == 0, theirs, mine)]
    )
    return (latent_out[None, None], text_out)


def solution(mesh):
    frames, heights, head = mesh.axis_names
    split = Mesh(
        mesh.devices.reshape(SIZES + (mesh.shape[head],)), AX + (head,)
    )
    tm, height = (("zh", "core"), ("x", "zl"))
    placed = (
        P(tm, height, None, None, head),
        P(None, tm, height, None, None, head),
        P(None, tm + height, None, head),
        P(tm, height, None, None),
        P(head),
    )
    return jax.shard_map(
        body,
        mesh=split,
        in_specs=placed,
        out_specs=(P(tm, height, None, None, head), P(None, head)),
        check_vma=False,
    )
```

time: 958 us -> 172 us (0.18); the launches traced: 941 us -> 171 us
  blocking collectives: 421 us -> 20.8 us
  other arithmetic: 184 us -> 9.15 us
  waiting for transfers between devices: 197 us -> 38.9 us
  local copies, waits for them, and re-layouts: 67.8 us -> 9.81 us
  starting transfers between devices: 9.31 us -> 60.4 us
  matrix products: 37.9 us -> 0 us
  Pallas kernels: 0 us -> 29.8 us
  between operations: 14.9 us -> 1.74 us
  loops' own time: 9.84 us -> 0 us
    all_gather x2 -> x0, blocking collectives: 421 us -> none  [combined_all(): gathered = jax.tree.map(lambda a: lax.all_gather(a, axis), part)]
    psum x1 -> x0, waiting for transfers between devices: 195 us -> none  [broadcast(): return lax.psum(kept, axis)]
    add x127 -> x0, other arithmetic: 152 us -> none  [the longest x64 80.8 us: combine(): merged_sum = sum_first * factor_first + sum_second * factor_second]
    dot_general x24 -> x0, matrix products: 37.9 us -> none  [the longest x6 12.7 us: one_head(): jnp.dot(weights.astype(jnp.bfloat16), head_value, preferred_element_type=...]
    pallas_call x0 -> x5, Pallas kernels: none -> 29.8 us  [the longest x2 15.6 us: rest_attention(): pl.pallas_call(functools.partial(rest_kernel, singles=len(ones), rows=row...]
    all_to_all x0 -> x4, starting transfers between devices: none -> 28.9 us  [the longest x2 15.3 us: spread(): lax.all_to_all(jnp.broadcast_to(chunk[None], (count,) + chunk.shape), axi...]
    ppermute x4 -> x13, starting transfers between devices: 9.23 us -> 31.5 us  [the longest x1 5.56 us: body(): x_far = lax.ppermute(far_pair, AX, X_FAR)]
    all_to_all x0 -> x4, waiting for transfers between devices: none -> 22.3 us  [the longest x2 20.2 us: spread(): lax.all_to_all(jnp.broadcast_to(chunk[None], (count,) + chunk.shape), axi...]
  transfers between devices with their start and end apart: 6 -> 17, of which waited for: 3 -> 5; matrix products, arithmetic and copies ran while one was open for 13% -> 8% of each run, Pallas kernels for 0% -> 17%
where the time goes in v1:
time: 172 us; the launch traced here: 171 us
  starting transfers between devices  60.4 us (35%)
  waiting for transfers between devices  38.9 us (23%)
  Pallas kernels  29.8 us (17%)
  blocking collectives  20.8 us (12%)
  local copies, waits for them, and re-layouts  9.81 us (6%)
  other arithmetic  9.15 us (5%)
  between operations  1.74 us (1%)
    all_to_all x1, blocking collectives, spread(): lax.all_to_all(jnp.broadcast_to(chunk[None], (count,) + chunk.shape), axi...  20.8 us
    all_to_all x2, waiting for transfers between devices, spread(): lax.all_to_all(jnp.broadcast_to(chunk[None], (count,) + chunk.shape), axi...  20.2 us
    pallas_call x2, Pallas kernels, rest_attention(): pl.pallas_call(functools.partial(rest_kernel, singles=len(ones), rows=row...  15.6 us
    all_to_all x2, starting transfers between devices, spread(): lax.all_to_all(jnp.broadcast_to(chunk[None], (count,) + chunk.shape), axi...  15.3 us
    ppermute x1, waiting for transfers between devices, body(): far_pair = lax.ppermute(pair, AX, SWAP_ZL)  14.6 us
    all_to_all x1, starting transfers between devices, body(): merged = merge_text(lax.all_to_all(parts, AX, 0, 0), heads, share)  9.12 us
    pallas_call x1, Pallas kernels, block_attention(): pl.pallas_call(functools.partial(block_kernel, rows=rows), grid=(columns...  8.37 us
    ppermute x1, starting transfers between devices, body(): x_far = lax.ppermute(far_pair, AX, X_FAR)  5.56 us
  transfers between devices with their start and end apart: 17, of which 5 were waited for; matrix products, arithmetic and copies ran while one was open for 8% of the time, Pallas kernels for 17%

profile of v1, /device:TPU:56, one launch (start us, length us, event | category | flops | bytes accessed | tf_op | source)
XLA Modules:
  0.0 170.5 jit_solution(16107705017192236053)
XLA Ops:
  0.6 1.4 dynamic-slice_bitcast_fusion.2
  2.0 1.9 %collective-permute-start.1 = (bf16[2,384,384]{2,1,0:T(8,128)(2,1)S(1)}, bf16[2,384,384]{2,1,0:T(8,128)(2,1)S(1)}, u32[]{:S(2)}, u32[]{:S(2)}) collective-permute-start(bf16[2,384,384]{2,1,0:T(8,128)(2,1)S(1)} %get-tuple-element.17), channel_id=1, source_target_pairs={{0,64},{8,72},{16,80},{24,88},{32,96},{40,104},{48,112},{56,120},{... | collective-permute-start | bytes 1769480 | tf_op jit(solution)/shard_map/ppermute | solution.py:275
  3.9 2.0 %collective-permute-done.1 = bf16[2,384,384]{2,1,0:T(8,128)(2,1)S(1)} collective-permute-done((bf16[2,384,384]{2,1,0:T(8,128)(2,1)S(1)}, bf16[2,384,384]{2,1,0:T(8,128)(2,1)S(1)}, u32[]{:S(2)}, u32[]{:S(2)}) %collective-permute-start.1) | collective-permute-done | bytes 589856 | tf_op jit(solution)/shard_map/ppermute | solution.py:275
  6.1 4.3 %collective-permute-start.2 = (bf16[2,2,384,384]{3,2,1,0:T(8,128)(2,1)S(1)}, bf16[2,2,384,384]{3,2,1,0:T(8,128)(2,1)}, u32[]{:S(2)}, u32[]{:S(2)}) collective-permute-start(bf16[2,2,384,384]{3,2,1,0:T(8,128)(2,1)S(1)} %pad_maximum_fusion.pair), channel_id=1, source_target_pairs={{0,8},{8,0},{16,24},{24,16},{32,40},{40,32},{48,56},{56,48},{64,72... | collective-permute-start | bytes 3538952 | tf_op jit(solution)/shard_map/ppermute | solution.py:277
  10.3 4.5 %all-to-all-start = ((bf16[16,24,384]{2,1,0:T(8,128)(2,1)}), bf16[16,24,384]{2,1,0:T(8,128)(2,1)}, u32[]{:S(2)}, u32[]{:S(2)}) async-start(bf16[16,24,384]{2,1,0:T(8,128)(2,1)} %bitcast.20), calls=%async_computation | async-start | bytes 589824 | tf_op jit(solution)/shard_map/all_to_all | solution.py:244
  15.0 1.2 maximum_maximum_fusion
  17.1 2.3 %collective-permute-start = (bf16[400,384]{1,0:T(8,128)(2,1)}, bf16[400,384]{1,0:T(8,128)(2,1)}, u32[]{:S(2)}, u32[]{:S(2)}) collective-permute-start(bf16[400,384]{1,0:T(8,128)(2,1)} %get-tuple-element.19), channel_id=1, source_target_pairs={{0,64},{8,0},{16,80},{24,16},{32,96},{40,32},{48,112},{56,48},{64,... | collective-permute-start | bytes 921608 | tf_op jit(solution)/shard_map/ppermute | solution.py:287
  20.1 1.1 fusion.1
  21.1 1.5 collective-permute-start.4
  22.6 14.6 %collective-permute-done.2.far_pair = bf16[2,2,384,384]{3,2,1,0:T(8,128)(2,1)} collective-permute-done((bf16[2,2,384,384]{3,2,1,0:T(8,128)(2,1)S(1)}, bf16[2,2,384,384]{3,2,1,0:T(8,128)(2,1)}, u32[]{:S(2)}, u32[]{:S(2)}) %collective-permute-start.2) | collective-permute-done | bytes 1179680 | tf_op jit(solution)/shard_map/ppermute | solution.py:277
  37.3 1.1 dynamic-slice_bitcast_fusion
  38.4 1.5 collective-permute-start.5
  39.9 2.1 %all-to-all-done = bf16[16,24,384]{2,1,0:T(8,128)(2,1)} async-done(((bf16[16,24,384]{2,1,0:T(8,128)(2,1)}), bf16[16,24,384]{2,1,0:T(8,128)(2,1)}, u32[]{:S(2)}, u32[]{:S(2)}) %all-to-all-start) | async-done | bytes 294944 | tf_op jit(solution)/shard_map/all_to_all | solution.py:244
  43.3 9.7 %all-to-all-start.1 = ((bf16[4,24,384]{2,1,0:T(8,128)(2,1)}), bf16[4,24,384]{2,1,0:T(8,128)(2,1)S(1)}, u32[]{:S(2)}, u32[]{:S(2)}) async-start(bf16[4,24,384]{2,1,0:T(8,128)(2,1)} %broadcast_in_dim.38), calls=%async_computation.1 | async-start | bytes 147456 | tf_op jit(solution)/shard_map/all_to_all | solution.py:238
  53.0 1.4 collective-permute-start.7
  54.3 1.3 collective-permute-start.8
  55.6 5.6 %collective-permute-start.3 = (bf16[2,2,384,384]{3,2,1,0:T(8,128)(2,1)}, bf16[2,2,384,384]{3,2,1,0:T(8,128)(2,1)}, u32[]{:S(2)}, u32[]{:S(2)}) collective-permute-start(bf16[2,2,384,384]{3,2,1,0:T(8,128)(2,1)} %collective-permute-done.2.far_pair), channel_id=1, source_target_pairs={{0,16},{16,32},{24,8},{32,48},{40,24},{56,40},{64,80},{80,96},{88,... | collective-permute-start | bytes 3538952 | tf_op jit(solution)/shard_map/ppermute | solution.py:294
  62.1 5.6 %all-to-all-start.2 = ((bf16[16,24,384]{2,1,0:T(8,128)(2,1)}), bf16[16,24,384]{2,1,0:T(8,128)(2,1)S(1)}, u32[]{:S(2)}, u32[]{:S(2)}) async-start(bf16[16,24,384]{2,1,0:T(8,128)(2,1)} %broadcast_in_dim.40), calls=%async_computation.2 | async-start | bytes 589824 | tf_op jit(solution)/shard_map/all_to_all | solution.py:238
  68.0 3.8 %collective-permute-start.6 = (bf16[2,384,384]{2,1,0:T(8,128)(2,1)}, bf16[2,384,384]{2,1,0:T(8,128)(2,1)S(1)}, u32[]{:S(2)}, u32[]{:S(2)}) collective-permute-start(bf16[2,384,384]{2,1,0:T(8,128)(2,1)} %collective-permute-done.4.refs_0_), channel_id=1, source_target_pairs={{0,16},{16,32},{24,8},{32,48},{40,24},{56,40},{64,80},{80,96},{88,... | collective-permute-start | bytes 1769480 | tf_op jit(solution)/shard_map/ppermute | solution.py:293
  71.8 1.3 collective-permute-start.9
  74.1 20.1 %all-to-all-done.2 = bf16[16,24,384]{2,1,0:T(8,128)(2,1)S(1)} async-done(((bf16[16,24,384]{2,1,0:T(8,128)(2,1)}), bf16[16,24,384]{2,1,0:T(8,128)(2,1)S(1)}, u32[]{:S(2)}, u32[]{:S(2)}) %all-to-all-start.2) | async-done | bytes 294944 | tf_op jit(solution)/shard_map/all_to_all | solution.py:238
  95.0 4.1 %text_partial.1 = (f32[3,128,128]{2,1,0:T(8,128)}, f32[128,128]{1,0:T(8,128)}) custom-call(s32[1]{0:T(128)} %bitcast.33.first, bf16[3,128,384]{2,1,0:T(8,128)(2,1)} %bitcast.66, bf16[2,2,384,384]{3,2,1,0:T(8,128)(2,1)} %bitcast.69), custom_call_target="tpu_custom_call" | custom-call | tf_op jit(solution)/shard_map/text_partial/pallas_call | solution.py:198
  100.1 1.6 pad_maximum_fusion.1
  101.7 9.1 %all-to-all-start.3 = ((f32[64,8,128]{2,1,0:T(8,128)}), f32[64,8,128]{2,1,0:T(8,128)S(1)}, u32[]{:S(2)}, u32[]{:S(2)}) async-start(f32[64,8,128]{2,1,0:T(8,128)} %pad_maximum_fusion.1), calls=%async_computation.3 | async-start | bytes 524288 | tf_op jit(solution)/shard_map/all_to_all | solution.py:340
  112.3 8.4 %block_attention.1 = (f32[384,384]{1,0:T(8,128)}, f32[384,384]{1,0:T(8,128)}, f32[384,384]{1,0:T(8,128)}, f32[384,384]{1,0:T(8,128)}) custom-call(s32[9]{0:T(128)} %convert_element_type.24.near_listed.listed, s32[9]{0:T(128)} %convert_element_type.25.far_listed.listed, bf16[400,384]{1,0:T(8,128)(2,1)} %copy-done.2, bf16[400,384]{1,0:T(8,128)(2,1)} %copy-done.3, ...), custom_call_target="tpu_custom_call" | custom-call | tf_op jit(solution)/shard_map/block_attention/pallas_call | solution.py:131
  120.7 7.8 %rest_far.1 = bf16[384,384]{1,0:T(8,128)(2,1)} custom-call(s32[9]{0:T(128)} %convert_element_type.25.far_listed.listed, bf16[400,384]{1,0:T(8,128)(2,1)} %copy-done.3, bf16[2,2,384,384]{3,2,1,0:T(8,128)(2,1)} %collective-permute-done.8.two, bf16[2,384,384]{2,1,0:T(8,128)(2,1)} %collective-permute-done.4.refs_0_, ...), custom_call_target="tpu_custom_call" | custom-call | tf_op jit(solution)/shard_map/rest_far/pallas_call | solution.py:145
  129.9 7.8 %rest_near.1 = bf16[384,384]{1,0:T(8,128)(2,1)} custom-call(s32[9]{0:T(128)} %convert_element_type.24.near_listed.listed, bf16[400,384]{1,0:T(8,128)(2,1)} %copy-done.2, bf16[2,2,384,384]{3,2,1,0:T(8,128)(2,1)} %collective-permute-done.3.two, bf16[2,384,384]{2,1,0:T(8,128)(2,1)} %collective-permute-done.4.refs_0_, ...), custom_call_target="tpu_custom_call" | custom-call | tf_op jit(solution)/shard_map/rest_near/pallas_call | solution.py:145
  137.7 1.3 collective-permute-start.11
  139.0 4.9 %collective-permute-start.12 = (bf16[384,384]{1,0:T(8,128)(2,1)S(1)}, bf16[384,384]{1,0:T(8,128)(2,1)S(1)}, u32[]{:S(2)}, u32[]{:S(2)}) collective-permute-start(bf16[384,384]{1,0:T(8,128)(2,1)S(1)} %copy-done.6), channel_id=1, source_target_pairs={{0,8},{16,24},{32,40},{48,56},{72,64},{88,80},{104,96},{120,112},{... | collective-permute-start | bytes 884744 | tf_op jit(solution)/shard_map/ppermute | solution.py:346
  144.6 1.8 %merge_text.1 = f32[2,384]{1,0:T(2,128)} custom-call(f32[64,8,128]{2,1,0:T(8,128)} %copy-done.4), custom_call_target="tpu_custom_call" | custom-call | tf_op jit(solution)/shard_map/merge_text/pallas_call | solution.py:229
  147.1 20.8 %all_to_all.25 = bf16[64,2,384]{2,1,0:T(2,128)(2,1)S(1)} all-to-all(bf16[64,2,384]{2,1,0:T(2,128)(2,1)S(1)} %broadcast_in_dim.42), channel_id=1, replica_groups=mesh['zh'=4,'core'=2,'x'=4,'zl'=2,'head'=8] {'zh','core','x','zl'}, dimensions={0} | all-to-all | bytes 196608 | tf_op jit(solution)/shard_map/all_to_all | solution.py:238
  168.6 1.1 select_bitcast_fusion.1
  (55 shorter events, 12.3 us)
Async XLA Ops:
  2.0 3.9 %collective-permute-start.1 = (bf16[2,384,384]{2,1,0:T(8,128)(2,1)S(1)}, bf16[2,384,384]{2,1,0:T(8,128)(2,1)S(1)}, u32[]{:S(2)}, u32[]{:S(2)}) collective-permute-start(bf16[2,384,384]{2,1,0:T(8,128)(2,1)S(1)} %get-tuple-element.17), channel_id=1, source_target_pairs={{0,64},{8,72},{16,80},{24,88},{32,96},{40,104},{48,112},{56,120},{... | collective-permute-start | bytes 1769480 | tf_op jit(solution)/shard_map/ppermute | solution.py:275
  5.9 8.9 %copy-start.7 = (s32[1,1,2,9]{3,2,1,0:T(2,128)S(1)}, s32[1,1,2,9]{3,2,1,0:T(2,128)}, u32[]{:S(2)}) copy-start(s32[1,1,2,9]{3,2,1,0:T(2,128)} %param.8) | copy-start | bytes 220
  6.0 48.3 %copy-start.1 = (bf16[2,2,384,384]{3,2,1,0:T(8,128)(2,1)}, bf16[2,2,384,384]{3,2,1,0:T(8,128)(2,1)S(1)}, u32[]{:S(2)}) copy-start(bf16[2,2,384,384]{3,2,1,0:T(8,128)(2,1)S(1)} %pad_maximum_fusion.pair) | copy-start | bytes 3538948
  6.1 31.2 %collective-permute-start.2 = (bf16[2,2,384,384]{3,2,1,0:T(8,128)(2,1)S(1)}, bf16[2,2,384,384]{3,2,1,0:T(8,128)(2,1)}, u32[]{:S(2)}, u32[]{:S(2)}) collective-permute-start(bf16[2,2,384,384]{3,2,1,0:T(8,128)(2,1)S(1)} %pad_maximum_fusion.pair), channel_id=1, source_target_pairs={{0,8},{8,0},{16,24},{24,16},{32,40},{40,32},{48,56},{56,48},{64,72... | collective-permute-start | bytes 3538952 | tf_op jit(solution)/shard_map/ppermute | solution.py:277
  10.3 31.6 %all-to-all-start = ((bf16[16,24,384]{2,1,0:T(8,128)(2,1)}), bf16[16,24,384]{2,1,0:T(8,128)(2,1)}, u32[]{:S(2)}, u32[]{:S(2)}) async-start(bf16[16,24,384]{2,1,0:T(8,128)(2,1)} %bitcast.20), calls=%async_computation | async-start | bytes 589824 | tf_op jit(solution)/shard_map/all_to_all | solution.py:244
  17.1 38.5 %collective-permute-start = (bf16[400,384]{1,0:T(8,128)(2,1)}, bf16[400,384]{1,0:T(8,128)(2,1)}, u32[]{:S(2)}, u32[]{:S(2)}) collective-permute-start(bf16[400,384]{1,0:T(8,128)(2,1)} %get-tuple-element.19), channel_id=1, source_target_pairs={{0,64},{8,0},{16,80},{24,16},{32,96},{40,32},{48,112},{56,48},{64,... | collective-permute-start | bytes 921608 | tf_op jit(solution)/shard_map/ppermute | solution.py:287
  21.1 46.9 %collective-permute-start.4 = (bf16[2,384,384]{2,1,0:T(8,128)(2,1)}, bf16[2,384,384]{2,1,0:T(8,128)(2,1)}, u32[]{:S(2)}, u32[]{:S(2)}) collective-permute-start(bf16[2,384,384]{2,1,0:T(8,128)(2,1)} %fusion.1), channel_id=1, source_target_pairs={{8,128},{24,144},{40,160},{56,176},{72,192},{88,208},{104,224},{12... | collective-permute-start | bytes 1769480 | tf_op jit(solution)/shard_map/ppermute | solution.py:279
  38.4 33.4 %collective-permute-start.5 = (bf16[2,384,384]{2,1,0:T(8,128)(2,1)S(1)}, bf16[2,384,384]{2,1,0:T(8,128)(2,1)}, u32[]{:S(2)}, u32[]{:S(2)}) collective-permute-start(bf16[2,384,384]{2,1,0:T(8,128)(2,1)S(1)} %dynamic-slice_bitcast_fusion), channel_id=1, source_target_pairs={{8,128},{24,144},{40,160},{56,176},{72,192},{88,208},{104,224},{12... | collective-permute-start | bytes 1769480 | tf_op jit(solution)/shard_map/ppermute | solution.py:295
  43.3 18.0 %all-to-all-start.1 = ((bf16[4,24,384]{2,1,0:T(8,128)(2,1)}), bf16[4,24,384]{2,1,0:T(8,128)(2,1)S(1)}, u32[]{:S(2)}, u32[]{:S(2)}) async-start(bf16[4,24,384]{2,1,0:T(8,128)(2,1)} %broadcast_in_dim.38), calls=%async_computation.1 | async-start | bytes 147456 | tf_op jit(solution)/shard_map/all_to_all | solution.py:238
  53.0 20.1 %collective-permute-start.7 = (bf16[400,384]{1,0:T(8,128)(2,1)}, bf16[400,384]{1,0:T(8,128)(2,1)}, u32[]{:S(2)}, u32[]{:S(2)}) collective-permute-start(bf16[400,384]{1,0:T(8,128)(2,1)} %get-tuple-element.18), channel_id=1, source_target_pairs={{8,64},{24,80},{40,96},{56,112},{64,8},{80,24},{96,40},{112,56},{1... | collective-permute-start | bytes 921608 | tf_op jit(solution)/shard_map/ppermute | solution.py:288
  54.3 66.3 %collective-permute-start.8 = (bf16[2,2,384,384]{3,2,1,0:T(8,128)(2,1)S(1)}, bf16[2,2,384,384]{3,2,1,0:T(8,128)(2,1)}, u32[]{:S(2)}, u32[]{:S(2)}) collective-permute-start(bf16[2,2,384,384]{3,2,1,0:T(8,128)(2,1)S(1)} %pad_maximum_fusion.pair), channel_id=1, source_target_pairs={{8,24},{16,0},{24,40},{32,16},{40,56},{48,32},{72,88},{80,64},{88,... | collective-permute-start | bytes 3538952 | tf_op jit(solution)/shard_map/ppermute | solution.py:278
  55.6 73.5 %collective-permute-start.3 = (bf16[2,2,384,384]{3,2,1,0:T(8,128)(2,1)}, bf16[2,2,384,384]{3,2,1,0:T(8,128)(2,1)}, u32[]{:S(2)}, u32[]{:S(2)}) collective-permute-start(bf16[2,2,384,384]{3,2,1,0:T(8,128)(2,1)} %collective-permute-done.2.far_pair), channel_id=1, source_target_pairs={{0,16},{16,32},{24,8},{32,48},{40,24},{56,40},{64,80},{80,96},{88,... | collective-permute-start | bytes 3538952 | tf_op jit(solution)/shard_map/ppermute | solution.py:294
  62.1 32.2 %all-to-all-start.2 = ((bf16[16,24,384]{2,1,0:T(8,128)(2,1)}), bf16[16,24,384]{2,1,0:T(8,128)(2,1)S(1)}, u32[]{:S(2)}, u32[]{:S(2)}) async-start(bf16[16,24,384]{2,1,0:T(8,128)(2,1)} %broadcast_in_dim.40), calls=%async_computation.2 | async-start | bytes 589824 | tf_op jit(solution)/shard_map/all_to_all | solution.py:238
  68.0 61.1 %collective-permute-start.6 = (bf16[2,384,384]{2,1,0:T(8,128)(2,1)}, bf16[2,384,384]{2,1,0:T(8,128)(2,1)S(1)}, u32[]{:S(2)}, u32[]{:S(2)}) collective-permute-start(bf16[2,384,384]{2,1,0:T(8,128)(2,1)} %collective-permute-done.4.refs_0_), channel_id=1, source_target_pairs={{0,16},{16,32},{24,8},{32,48},{40,24},{56,40},{64,80},{80,96},{88,... | collective-permute-start | bytes 1769480 | tf_op jit(solution)/shard_map/ppermute | solution.py:293
  71.8 48.9 %collective-permute-start.9 = (bf16[2,384,384]{2,1,0:T(8,128)(2,1)}, bf16[2,384,384]{2,1,0:T(8,128)(2,1)}, u32[]{:S(2)}, u32[]{:S(2)}) collective-permute-start(bf16[2,384,384]{2,1,0:T(8,128)(2,1)} %collective-permute-done.5.refs_1_), channel_id=1, source_target_pairs={{8,24},{16,0},{24,40},{32,16},{40,56},{48,32},{72,88},{80,64},{88,... | collective-permute-start | bytes 1769480 | tf_op jit(solution)/shard_map/ppermute | solution.py:296
  74.1 38.1 %copy-start.2 = (bf16[400,384]{1,0:T(8,128)(2,1)}, bf16[400,384]{1,0:T(8,128)(2,1)S(1)}, u32[]{:S(2)}) copy-start(bf16[400,384]{1,0:T(8,128)(2,1)S(1)} %get-tuple-element.21.near_q.query) | copy-start | bytes 921604
  74.1 38.1 %copy-start.3 = (bf16[400,384]{1,0:T(8,128)(2,1)}, bf16[400,384]{1,0:T(8,128)(2,1)S(1)}, u32[]{:S(2)}) copy-start(bf16[400,384]{1,0:T(8,128)(2,1)S(1)} %get-tuple-element.20.far_q.query) | copy-start | bytes 921604
  94.2 0.7 copy-start
  101.7 42.2 %all-to-all-start.3 = ((f32[64,8,128]{2,1,0:T(8,128)}), f32[64,8,128]{2,1,0:T(8,128)S(1)}, u32[]{:S(2)}, u32[]{:S(2)}) async-start(f32[64,8,128]{2,1,0:T(8,128)} %pad_maximum_fusion.1), calls=%async_computation.3 | async-start | bytes 524288 | tf_op jit(solution)/shard_map/all_to_all | solution.py:340
  128.4 40.2 %collective-permute-start.10 = (bf16[384,384]{1,0:T(8,128)(2,1)}, bf16[384,384]{1,0:T(8,128)(2,1)S(1)}, u32[]{:S(2)}, u32[]{:S(2)}) collective-permute-start(bf16[384,384]{1,0:T(8,128)(2,1)} %rest_far.1), channel_id=1, source_target_pairs={{8,64},{24,80},{40,96},{56,112},{64,8},{80,24},{96,40},{112,56},{1... | collective-permute-start | bytes 884744 | tf_op jit(solution)/shard_map/ppermute | solution.py:347
  129.1 0.8 copy-start.5
  129.9 9.1 %copy-start.6 = (bf16[384,384]{1,0:T(8,128)(2,1)S(1)}, bf16[384,384]{1,0:T(8,128)(2,1)}, u32[]{:S(2)}) copy-start(bf16[384,384]{1,0:T(8,128)(2,1)} %rest_far.1) | copy-start | bytes 884740
  137.7 30.8 %collective-permute-start.11 = (bf16[384,384]{1,0:T(8,128)(2,1)}, bf16[384,384]{1,0:T(8,128)(2,1)S(1)}, u32[]{:S(2)}, u32[]{:S(2)}) collective-permute-start(bf16[384,384]{1,0:T(8,128)(2,1)} %rest_near.1), channel_id=1, source_target_pairs={{8,72},{24,88},{40,104},{56,120},{64,0},{80,16},{96,32},{112,48},{... | collective-permute-start | bytes 884744 | tf_op jit(solution)/shard_map/ppermute | solution.py:351
  139.0 29.5 %collective-permute-start.12 = (bf16[384,384]{1,0:T(8,128)(2,1)S(1)}, bf16[384,384]{1,0:T(8,128)(2,1)S(1)}, u32[]{:S(2)}, u32[]{:S(2)}) collective-permute-start(bf16[384,384]{1,0:T(8,128)(2,1)S(1)} %copy-done.6), channel_id=1, source_target_pairs={{0,8},{16,24},{32,40},{48,56},{72,64},{88,80},{104,96},{120,112},{... | collective-permute-start | bytes 884744 | tf_op jit(solution)/shard_map/ppermute | solution.py:346
  143.9 0.7 copy-start.4
